TPU v7x, 256 devices: a whole 4x4x8 slice. The times are simulated.
256 devices in a mesh: panel: 32 (over z, y_lo, core), rep: 8 (over x, y_hi).
Axes of the slice: x: 4, y: 4 (y_hi: 2, y_lo: 2; y = y_hi * 2 + y_lo), z: 8, core: 2. Of those that a mesh axis runs over, the one named last changes fastest.
Arguments:
- x_src: bfloat16 [4096, 128], P('panel'), may hold values from -6 to 6
- x_dst: bfloat16 [131072, 128], P(('panel', 'rep')), may hold values from -6 to 6
- weight: bfloat16 [128, 512], replicated, may hold values from -0.5 to 0.5
- att_src: float32 [8, 64], replicated, may hold values from -0.75 to 0.75
- att_dst: float32 [8, 64], replicated, may hold values from -0.75 to 0.75
- grad_out: bfloat16 [131072, 512], P(('panel', 'rep')), may hold values from -6 to 6
- block_rows: int32 [4096], P(('panel', 'rep')), may hold values from 0 to 3, as said below
- block_cols: int32 [4096], P(('panel', 'rep')), may hold values from 0 to 31
- block_masks: int32 [4096, 128, 128], P(('panel', 'rep')), may hold values from 0 to 1, as said below
- block_counts: int32 [256], P(('panel', 'rep')), may hold values from 2 to 16, as said below
Outputs:
- grad_src: float32 [4096, 128], P('panel')
- grad_dst: float32 [131072, 128], P(('panel', 'rep'))
- grad_weight: float32 [128, 512], replicated
- grad_att_src: float32 [8, 64], replicated
- grad_att_dst: float32 [8, 64], replicated
Inputs may be any that keep to these rules, and one draw needn't show every extreme that they name: `block_counts`: live block slots of one device; at least one device has exactly 16. The pairs of block_rows and block_cols within one device's 16 slots are distinct. `block_masks`: slots at or after a device's count of live blocks hold only zeros.
All inputs are finite; a program needn't handle non-finite values.
Results may differ from a plain program's by a relative error of at most 0.012.
The roundings to bfloat16 on the way count: a program that leaves them out, or rounds other values in their place, can miss the bound.
Values may be sent and summed in bfloat16 or wider, within the bound.
No kernel may reach another device: no remote copies, remote signals or barrier semaphores. Data moves between devices by JAX's collectives and lax.ppermute only.
A program may use at most 128 MiB of HBM per device.

v0:
```python
import math
import jax
import jax.numpy as jnp
from jax import lax
from jax.sharding import PartitionSpec as P

HIGHEST_PRECISION = lax.Precision.HIGHEST


def smooth_leaky(values):
    return 0.2 * values + 0.8 * jax.nn.softplus(values)


def smooth_slope(values):
    return 0.2 + 0.8 * jax.nn.sigmoid(values)


def shards(
    x_src,
    x_dst,
    weight,
    att_src,
    att_dst,
    grad_out,
    block_rows,
    block_cols,
    block_masks,
    block_counts,
):
    num_heads, head_dim = att_src.shape
    model_width = weight.shape[1]
    block_size = block_masks.shape[1]
    dest_count = x_dst.shape[0]
    source_local = x_src.shape[0]
    slot_count = block_rows.shape[0]
    proj_own = jnp.dot(x_src, weight, preferred_element_type=jnp.float32).astype(jnp.bfloat16)
    proj_all = lax.all_gather(proj_own, "panel", axis=0, tiled=True)
    source_total = proj_all.shape[0]
    dest_blocks = dest_count // block_size
    source_blocks = source_total // block_size
    source_feats = proj_all.reshape(source_total, num_heads, head_dim)
    score_src = jnp.einsum(
        "jhk,hk->hj", source_feats.astype(jnp.float32), att_src, precision=HIGHEST_PRECISION
    )
    proj_dst = jnp.dot(x_dst, weight, preferred_element_type=jnp.float32).astype(jnp.bfloat16)
    feats = proj_dst.reshape(dest_count, num_heads, head_dim)
    feats_wide = feats.astype(jnp.float32)
    score_d = jnp.einsum("ihk,hk->hi", feats_wide, att_dst, precision=HIGHEST_PRECISION)
    score_own = jnp.einsum("ihk,hk->hi", feats_wide, att_src, precision=HIGHEST_PRECISION)
    cotan = grad_out.reshape(dest_count, num_heads, head_dim)
    cotan_wide = cotan.astype(jnp.float32)
    live_count = block_counts[0]
    score_d_blocks = score_d.reshape(num_heads, dest_blocks, block_size)
    score_src_blocks = score_src.reshape(num_heads, source_blocks, block_size)
    source_row_blocks = source_feats.reshape(source_blocks, block_size, num_heads, head_dim)
    cotan_blocks = cotan.reshape(dest_blocks, block_size, num_heads, head_dim)
    group = math.gcd(slot_count, 16)
    groups = slot_count // group
    alive_all = (jnp.arange(slot_count, dtype=jnp.int32) < live_count).astype(jnp.float32)
    slot_inputs = (
        block_rows.reshape(groups, group),
        block_cols.reshape(groups, group),
        block_masks.reshape(groups, group, block_size, block_size),
        alive_all.reshape(groups, group),
    )

    def group_scores(rows, cols, masks, alive):
        dest_hot = (rows[:, None] == jnp.arange(dest_blocks, dtype=jnp.int32)[None, :]).astype(
            jnp.float32
        )
        source_hot = (cols[:, None] == jnp.arange(source_blocks, dtype=jnp.int32)[None, :]).astype(
            jnp.float32
        )
        score_rows = jnp.einsum(
            "gd,hdu->ghu", dest_hot, score_d_blocks, precision=HIGHEST_PRECISION
        )
        score_cols = jnp.einsum(
            "gs,hsv->ghv", source_hot, score_src_blocks, precision=HIGHEST_PRECISION
        )
        pre_score = score_rows[:, :, :, None] + score_cols[:, :, None, :]
        edge_mask = masks.astype(jnp.float32) * alive[:, None, None]
        edge_weight = jnp.exp(smooth_leaky(pre_score)) * edge_mask[:, None]
        source_rows = jnp.take(source_row_blocks, cols, axis=0)
        return (dest_hot, source_hot, pre_score, edge_weight, source_rows)

    def forward_group(carried_fwd, slot_group):
        denominator, numerator = carried_fwd
        rows, cols, masks, alive = slot_group
        dest_hot, source_hot, pre_score, edge_weight, source_rows = group_scores(
            rows, cols, masks, alive
        )
        part_num = jnp.einsum(
            "ghij,gjhk->gihk",
            edge_weight.astype(jnp.bfloat16),
            source_rows,
            preferred_element_type=jnp.float32,
        )
        denominator = denominator + jnp.einsum(
            "gd,ghi->hdi", dest_hot, edge_weight.sum(axis=3), precision=HIGHEST_PRECISION
        )
        numerator = numerator + jnp.einsum(
            "gd,gihk->dihk", dest_hot, part_num, precision=HIGHEST_PRECISION
        )
        return ((denominator, numerator), None)

    (denominator_blocks, numerator_blocks), _ = lax.scan(
        forward_group,
        (
            jnp.zeros((num_heads, dest_blocks, block_size), jnp.float32),
            jnp.zeros((dest_blocks, block_size, num_heads, head_dim), jnp.float32),
        ),
        slot_inputs,
    )
    denominator = denominator_blocks.reshape(num_heads, dest_count)
    numerator = numerator_blocks.reshape(dest_count, num_heads, head_dim)
    pre_self = score_d + score_own
    self_weight = jnp.exp(smooth_leaky(pre_self))
    denominator = denominator + self_weight
    numerator = numerator + self_weight.T[:, :, None] * feats_wide
    attended = numerator / denominator.T[:, :, None]
    centred = jnp.sum(cotan_wide * attended, axis=2).T
    denominator_full = denominator.reshape(num_heads, dest_blocks, block_size)
    centred_full = centred.reshape(num_heads, dest_blocks, block_size)

    def backward_group(carried_bwd, slot_group):
        grad_source, grad_score_src, grad_score_dst = carried_bwd
        rows, cols, masks, alive = slot_group
        dest_hot, source_hot, pre_score, edge_weight, source_rows = group_scores(
            rows, cols, masks, alive
        )
        denom_rows = jnp.einsum(
            "gd,hdi->ghi", dest_hot, denominator_full, precision=HIGHEST_PRECISION
        )
        attention = edge_weight / denom_rows[:, :, :, None]
        cotan_rows = jnp.take(cotan_blocks, rows, axis=0)
        pair_grad = jnp.einsum(
            "gihk,gjhk->ghij", cotan_rows, source_rows, preferred_element_type=jnp.float32
        )
        centred_rows = jnp.einsum(
            "gd,hdi->ghi", dest_hot, centred_full, precision=HIGHEST_PRECISION
        )
        score_grad = attention * (pair_grad - centred_rows[:, :, :, None]) * smooth_slope(pre_score)
        feat_grad = jnp.einsum(
            "ghij,gihk->gjhk",
            attention.astype(jnp.bfloat16),
            cotan_rows,
            preferred_element_type=jnp.float32,
        )
        grad_source = grad_source + jnp.einsum(
            "gs,gjhk->sjhk", source_hot, feat_grad, precision=HIGHEST_PRECISION
        )
        grad_score_src = grad_score_src + jnp.einsum(
            "gs,ghj->hsj", source_hot, score_grad.sum(axis=2), precision=HIGHEST_PRECISION
        )
        grad_score_dst = grad_score_dst + jnp.einsum(
            "gd,ghi->hdi", dest_hot, score_grad.sum(axis=3), precision=HIGHEST_PRECISION
        )
        return ((grad_source, grad_score_src, grad_score_dst), None)

    (grad_source_blocks, grad_score_src_blocks, grad_score_dst_blocks), _ = lax.scan(
        backward_group,
        (
            jnp.zeros((source_blocks, block_size, num_heads, head_dim), jnp.float32),
            jnp.zeros((num_heads, source_blocks, block_size), jnp.float32),
            jnp.zeros((num_heads, dest_blocks, block_size), jnp.float32),
        ),
        slot_inputs,
    )
    grad_source = grad_source_blocks.reshape(source_total, num_heads, head_dim)
    grad_score_src = grad_score_src_blocks.reshape(num_heads, source_total)
    grad_score_dst = grad_score_dst_blocks.reshape(num_heads, dest_count)
    self_attention = self_weight / denominator
    self_pair = jnp.sum(cotan_wide * feats_wide, axis=2).T
    self_grad = self_attention * (self_pair - centred) * smooth_slope(pre_self)
    grad_score_dst = grad_score_dst + self_grad
    grad_dest = (
        self_attention.T[:, :, None] * cotan_wide
        + self_grad.T[:, :, None] * att_src[None]
        + grad_score_dst.T[:, :, None] * att_dst[None]
    )
    grad_source = grad_source + grad_score_src.T[:, :, None] * att_src[None]
    att_src_part = jnp.einsum(
        "hj,jhk->hk", grad_score_src, source_feats.astype(jnp.float32), precision=HIGHEST_PRECISION
    ) + jnp.einsum("hi,ihk->hk", self_grad, feats_wide, precision=HIGHEST_PRECISION)
    att_dst_part = jnp.einsum("hi,ihk->hk", grad_score_dst, feats_wide, precision=HIGHEST_PRECISION)
    weight_t = weight.astype(jnp.float32).T
    source_flat = grad_source.reshape(source_total, model_width)
    dest_flat = grad_dest.reshape(dest_count, model_width)
    grad_dst = jnp.dot(dest_flat, weight_t, precision=HIGHEST_PRECISION)
    weight_part = jnp.dot(x_dst.astype(jnp.float32).T, dest_flat, precision=HIGHEST_PRECISION)
    share_rows = source_local // lax.axis_size("rep")
    share_start = lax.axis_index("rep") * share_rows
    panel_part = lax.psum_scatter(source_flat, "panel", scatter_dimension=0, tiled=True)
    panel_sum = lax.psum(panel_part, "rep")
    own_share = lax.dynamic_slice_in_dim(panel_sum, share_start, share_rows, 0)
    grad_src = jnp.dot(panel_sum, weight_t, precision=HIGHEST_PRECISION)
    own_inputs = lax.dynamic_slice_in_dim(x_src, share_start, share_rows, 0).astype(jnp.float32)
    weight_part = weight_part + jnp.dot(own_inputs.T, own_share, precision=HIGHEST_PRECISION)
    grad_weight, grad_att_src, grad_att_dst = lax.psum(
        (weight_part, att_src_part, att_dst_part), ("panel", "rep")
    )
    return (grad_src, grad_dst, grad_weight, grad_att_src, grad_att_dst)


def solution(mesh):
    return jax.shard_map(
        shards,
        mesh=mesh,
        in_specs=(
            P("panel", None),
            P(("panel", "rep"), None),
            P(),
            P(),
            P(),
            P(("panel", "rep"), None),
            P(("panel", "rep")),
            P(("panel", "rep")),
            P(("panel", "rep"), None, None),
            P(("panel", "rep")),
        ),
        out_specs=(P("panel", None), P(("panel", "rep"), None), P(), P(), P()),
        check_vma=False,
    )
```

profile of v0, /device:TPU:2, one launch (start us, length us, event | category | flops | bytes accessed | tf_op | source)
XLA Modules:
  0.0 674.6 jit_solution(18316904664663348412)
XLA Ops:
  7.3 0.8 copy-done
  8.1 1.6 convolution_convert_fusion.1
  9.7 2.1 copy.48
  11.8 1.6 reshape.148
  13.4 1.2 convolution_convert_fusion
  14.7 1.0 fusion.98
  15.7 0.9 fusion.94
  17.3 0.6 copy.39
  17.9 0.8 mul.185
  18.7 0.7 compare_select_fusion.3
  19.4 0.9 gather_fusion
  20.4 0.3 fusion.100
  20.7 2.4 convert_multiply_fusion.2
  23.1 57.2 %all-gather.2.cloned.1.call-done = bf16[4096,512]{1,0:T(8,128)(2,1)} async-done(((bf16[128,512]{1,0:T(8,128)(2,1)}), bf16[4096,512]{1,0:T(8,128)(2,1)}) %all-gather.2.cloned.1.call-update) | async-done | bytes 4194320 | tf_op jit(solution)/shard_map/all_gather | solution.py:37
  80.3 6.4 copy.41
  86.7 3.9 fusion.99
  90.7 0.2 fusion.38
  91.0 9.5 %fusion.23 = f32[16,8,128]{2,1,0:T(8,128)S(1)} fusion(f32[16,128,128]{2,1,0:T(8,128)} %convert_multiply_fusion.2, f32[16,8,128]{2,1,0:T(8,128)S(1)} %copy.42, f32[16,8,128]{2,1,0:T(8,128)S(1)} %copy.40), kind=kLoop, calls=%fused_computation.33 | loop fusion | flops 25149440 | bytes 1245184 | tf_op jit(solution)/shard_map/while/body/eval_jaxpr/reduce_sum | solution.py:99
  100.4 0.1 convolution_bitcast_fusion.2
  100.7 11.2 %reshape.149 = bf16[32,128,8,64]{3,2,1,0:T(8,128)(2,1)} reshape(bf16[4096,512]{1,0:T(8,128)(2,1)} %all-gather.2.cloned.1.call-done) | data formatting | bytes 8388608 | tf_op jit(solution)/shard_map/reshape;reshape | solution.py:55
  111.8 9.1 %copy.47 = bf16[32,128,8,64]{1,3,2,0:T(8,128)(2,1)} copy(bf16[32,128,8,64]{3,2,1,0:T(8,128)(2,1)} %reshape.149) | data formatting | bytes 8388608 | tf_op jit(solution)/shard_map/reshape;reshape | solution.py:55
  120.9 4.3 gather_fusion.1
  125.3 9.9 %fusion.27 = f32[16,128,8,64]{1,3,2,0:T(8,128)S(1)} fusion(f32[16,128,128]{2,1,0:T(8,128)} %convert_multiply_fusion.2, f32[16,8,128]{2,1,0:T(8,128)S(1)} %copy.42, f32[16,8,128]{2,1,0:T(8,128)S(1)} %copy.40, bf16[16,128,8,64]{1,3,2,0:T(8,128)(2,1)} %gather_fusion.1, pred[16]{0:T(512)(128)(4,1)S(1)} %get-tuple-element.104), kind=kOutput, calls=%fused_computation.35 | convolution fusion | flops 294649856 | bytes 7471120 | tf_op jit(solution)/shard_map/while/body/eval_jaxpr/ghij,gjhk->gihk/dot_general | solution.py:92
  135.1 5.0 fusion.14
  140.1 2.6 reshape.108
  142.8 1.6 fusion.33
  144.4 0.2 fusion.89
  144.6 0.2 fusion.91
  144.9 11.8 %fusion.24 = f32[16,128,8,64]{1,3,2,0:T(8,128)S(1)} fusion(f32[16,8,128]{2,1,0:T(8,128)S(1)} %copy.44, f32[16,128,128]{2,1,0:T(8,128)} %convert_multiply_fusion.2, f32[16,8,128]{2,1,0:T(8,128)S(1)} %copy.42, f32[16,8,128]{2,1,0:T(8,128)S(1)} %copy.40, bf16[16,128,8,64]{1,3,2,0:T(8,128)(2,1)S(1)} %gather_fusion, pred[16]{0:T(512)(128)(4,1)S(1)} %get-tuple-element.105), kind=kOutput, calls=%fused_computation.34 | convolution fusion | flops 296747008 | bytes 7536656 | tf_op jit(solution)/shard_map/while/body/eval_jaxpr/ghij,gihk->gjhk/dot_general | solution.py:143
  156.7 15.4 %fusion.96 = (f32[16,8,128]{2,1,0:T(8,128)S(1)}, f32[16,8,128]{2,1,0:T(8,128)S(1)}) fusion(f32[16,8,128]{2,1,0:T(8,128)S(1)} %copy.50, bf16[16,128,8,64]{1,3,2,0:T(8,128)(2,1)S(1)} %copy-done.1, pred[16]{0:T(512)(128)(4,1)S(1)} %get-tuple-element.104, bf16[16,128,8,64]{1,3,2,0:T(8,128)(2,1)S(1)} %gather_fusion, pred[16]{0:T(512)(128)(4,1)S(1)} %get-tuple-element.105, ...), kind=kOutput, calls=%fused_computation.128 | convolution fusion | flops 316637184 | bytes 5636128 | tf_op jit(solution)/shard_map/while/body/eval_jaxpr/gihk,gjhk->ghij/dot_general | solution.py:136
  172.2 0.3 fusion.42
  172.6 5.8 fusion.16
  178.4 12.0 %bitcast_add_fusion = f32[4096,512]{0,1:T(8,128)} fusion(f32[64,8,32,128]{3,2,1,0:T(8,128)S(1)} %bitcast.176, f32[512]{0:T(512)S(1)} %mul.185, f32[4096,8]{0,1:T(8,128)S(1)} %bitcast.183), kind=kLoop, calls=%fused_computation.22 | loop fusion | flops 4194304 | bytes 16910336 | tf_op jit(solution)/shard_map/add | solution.py:181
  190.5 0.6 copy-done.8
  191.2 0.1 convolution_bitcast_fusion.1
  191.5 0.3 fusion.34
  191.8 0.5 fusion.59
  192.3 0.6 convolution_bitcast_fusion
  192.9 5.1 fusion.103
  198.0 122.5 %reduce-scatter.2.cloned.1.call-done = f32[128,512]{0,1:T(8,128)} async-done(((f32[4096,512]{0,1:T(8,128)}), f32[128,512]{0,1:T(8,128)}) %reduce-scatter.2.cloned.1.call-update) | async-done | bytes 262160 | tf_op jit(solution)/shard_map/reduce_scatter | solution.py:193
  320.5 0.5 fusion.57
  321.0 75.9 %all-reduce = (f32[8,64]{1,0:T(8,128)}, f32[8,64]{1,0:T(8,128)}) all-reduce(f32[8,64]{1,0:T(8,128)S(1)} %add.168, f32[8,64]{1,0:T(8,128)S(1)} %bitcast.197), channel_id=1, replica_groups=mesh['panel'=32,'rep'=8] {'panel','rep'}, use_global_device_ids=true, to_apply=%region_8.10 | all-reduce | flops 1024 | bytes 8192 | tf_op jit(solution)/shard_map/psum | solution.py:199
  396.9 1.7 fusion.102
  398.6 11.2 %all-reduce.4.cloned.1.call-done = f32[128,512]{0,1:T(8,128)} async-done(((f32[128,512]{0,1:T(8,128)}), f32[128,512]{0,1:T(8,128)}) %all-reduce.4.cloned.1.call-update) | async-done | bytes 262160 | tf_op jit(solution)/shard_map/psum | solution.py:194
  409.9 2.0 convolution_add_fusion
  411.9 2.0 fusion.101
  413.8 252.2 %all-reduce.6.cloned.1.call-done = f32[128,512]{0,1:T(8,128)} async-done(((f32[128,512]{0,1:T(8,128)}), f32[128,512]{0,1:T(8,128)}) %all-reduce.6.cloned.1.call-update) | async-done | bytes 262160 | tf_op jit(solution)/shard_map/psum | solution.py:199
  666.1 1.8 copy.54
  (47 shorter events, 0.9 us)
Async XLA Ops:
  7.2 0.9 copy-start
  7.2 13.2 %copy-start.7 = (s32[16]{0:T(128)S(1)}, s32[16]{0:T(128)}, u32[]{:S(2)}) copy-start(s32[16]{0:T(128)} %param.18) | copy-start | bytes 196
  7.2 13.2 %copy-start.6 = (f32[8,64]{1,0:T(8,128)S(1)}, f32[8,64]{1,0:T(8,128)}, u32[]{:S(2)}) copy-start(f32[8,64]{1,0:T(8,128)} %param.15) | copy-start | bytes 6148
  7.2 13.1 %copy-start.9 = (s32[16]{0:T(128)S(1)}, s32[16]{0:T(128)}, u32[]{:S(2)}) copy-start(s32[16]{0:T(128)} %param.19) | copy-start | bytes 196
  7.2 73.1 %all-gather.2.cloned.1.call-start = ((), (), s32[]{:S(2)}) async-start(), calls=%async_computation.1 | async-start | bytes 4325376 | tf_op jit(solution)/shard_map/all_gather | solution.py:37
  9.7 310.8 %reduce-scatter.2.cloned.1.call-start = ((), (), s32[]{:S(2)}) async-start(), calls=%async_computation.2 | async-start | bytes 8650752 | tf_op jit(solution)/shard_map/reduce_scatter | solution.py:193
  125.2 17.5 %copy-start.2 = (bf16[512,512]{0,1:T(8,128)(2,1)S(1)}, bf16[512,512]{0,1:T(8,128)(2,1)}, u32[]{:S(2)}) copy-start(bf16[512,512]{0,1:T(8,128)(2,1)} %copy.48) | copy-start | bytes 1572868
  144.9 11.8 %copy-start.1 = (bf16[16,128,8,64]{1,3,2,0:T(8,128)(2,1)S(1)}, bf16[16,128,8,64]{1,3,2,0:T(8,128)(2,1)}, u32[]{:S(2)}) copy-start(bf16[16,128,8,64]{1,3,2,0:T(8,128)(2,1)} %gather_fusion.1) | copy-start | bytes 6291460
  144.9 11.8 %copy-start.4 = (f32[16,128,128]{2,1,0:T(8,128)S(1)}, f32[16,128,128]{2,1,0:T(8,128)}, u32[]{:S(2)}) copy-start(f32[16,128,128]{2,1,0:T(8,128)} %convert_multiply_fusion.2) | copy-start | bytes 3145732
  190.4 0.7 copy-start.8
  190.4 1.1 copy-start.3
  190.4 1.8 copy-start.5
  190.5 219.4 %all-reduce.4.cloned.1.call-start = ((), (), s32[]{:S(2)}) async-start(), calls=%async_computation.3 | async-start | bytes 524288 | tf_op jit(solution)/shard_map/psum | solution.py:194
  320.5 345.6 %all-reduce.6.cloned.1.call-start = ((), (), s32[]{:S(2)}) async-start(), calls=%async_computation.4 | async-start | bytes 524288 | tf_op jit(solution)/shard_map/psum | solution.py:199
Sparse Core Ops, SparseCore 0:
  10.5 69.7 all-gather.1
  190.6 129.8 reduce-scatter.1
  323.1 86.7 all-reduce.3
  416.6 249.4 all-reduce.5
where the time goes:
time: 682 us; the launch traced here: 675 us
  waiting for transfers between devices  443 us (65%)
  blocking collectives  75.9 us (11%)
  matrix products  70.5 us (10%)
  local copies, waits for them, and re-layouts  43.3 us (6%)
  other arithmetic  26.5 us (4%)
  between operations  15 us (2%)
    psum x1, waiting for transfers between devices, shards(): lax.psum((weight_part, att_src_part, att_dst_part), ('panel', 'rep'))  252 us
    reduce_scatter x1, waiting for transfers between devices, shards(): lax.psum_scatter(source_flat, 'panel', scatter_dimension=0, tiled=True)  122 us
    psum x1, blocking collectives, shards(): lax.psum((weight_part, att_src_part, att_dst_part), ('panel', 'rep'))  75.9 us
    all_gather x1, waiting for transfers between devices, shards(): proj_all = lax.all_gather(proj_own, 'panel', axis=0, tiled=True)  57.2 us
    another operation x2, local copies, waits for them, and re-layouts, shards(): source_feats.reshape(source_blocks, block_size, num_heads, head_dim)  20.2 us
    dot_general x1, matrix products, backward_group(): jnp.einsum('gihk,gjhk->ghij', cotan_rows, source_rows, preferred_element_...  15.4 us
  transfers between devices with their start and end apart: 4, of which 4 were waited for; matrix products, arithmetic and copies ran while one was open for 3% of the time, Pallas kernels for 0%

commit v1 on v0

--- a/solution.py
+++ b/solution.py
@@ -34,7 +34,9 @@
     source_local = x_src.shape[0]
     slot_count = block_rows.shape[0]
     proj_own = jnp.dot(x_src, weight, preferred_element_type=jnp.float32).astype(jnp.bfloat16)
-    proj_all = lax.all_gather(proj_own, "panel", axis=0, tiled=True)
+    proj_all = jnp.concatenate(
+        lax.all_to_all(jnp.stack([proj_own] * lax.axis_size("panel")), "panel", 0, 0), axis=0
+    )
     source_total = proj_all.shape[0]
     dest_blocks = dest_count // block_size
     source_blocks = source_total // block_size

time: 682 us -> 705 us (1.034)
  waiting for transfers between devices: 443 us -> 472 us
  local copies, waits for them, and re-layouts: 43.3 us -> 31.6 us
  starting transfers between devices: 0.16 us -> 10.1 us
    all_to_all x0 -> x1, waiting for transfers between devices: none -> 89 us  [shards(): lax.all_to_all(jnp.stack([proj_own] * lax.axis_size('panel')), 'panel', 0...]
    all_gather x1 -> x0, waiting for transfers between devices: 57.2 us -> none  [shards(): proj_all = lax.all_gather(proj_own, 'panel', axis=0, tiled=True)]
    all_to_all x0 -> x1, starting transfers between devices: none -> 9.99 us  [shards(): lax.all_to_all(jnp.stack([proj_own] * lax.axis_size('panel')), 'panel', 0...]
    another operation x2, local copies, waits for them, and re-layouts: 20.2 us -> 10.7 us  [the longest x1 7.74 us: shards(): source_feats = proj_all.reshape(source_total, num_heads, head_dim)]
where the time goes in v1:
time: 705 us; the launch traced here: 698 us
  waiting for transfers between devices  472 us (67%)
  blocking collectives  75.2 us (11%)
  matrix products  68 us (10%)
  local copies, waits for them, and re-layouts  31.6 us (4%)
  other arithmetic  25.9 us (4%)
  between operations  15.1 us (2%)
  starting transfers between devices  10.1 us (1%)
    psum x1, waiting for transfers between devices, shards(): lax.psum((weight_part, att_src_part, att_dst_part), ('panel', 'rep'))  252 us
    reduce_scatter x1, waiting for transfers between devices, shards(): lax.psum_scatter(source_flat, 'panel', scatter_dimension=0, tiled=True)  119 us
    all_to_all x1, waiting for transfers between devices, shards(): lax.all_to_all(jnp.stack([proj_own] * lax.axis_size('panel')), 'panel', 0...  89 us
    psum x1, blocking collectives, shards(): lax.psum((weight_part, att_src_part, att_dst_part), ('panel', 'rep'))  75.2 us
    dot_general x1, matrix products, backward_group(): jnp.einsum('gihk,gjhk->ghij', cotan_rows, source_rows, preferred_element_...  16.1 us
  transfers between devices with their start and end apart: 4, of which 4 were waited for; matrix products, arithmetic and copies ran while one was open for 3% of the time, Pallas kernels for 0%

profile of v1, /device:TPU:2, one launch (start us, length us, event | category | flops | bytes accessed | tf_op | source)
XLA Modules:
  0.0 698.4 jit_solution(13731058129409394105)
XLA Ops:
  7.2 0.9 copy-done
  8.1 0.9 convolution_convert_fusion.1
  9.0 0.1 copy.40
  9.2 2.9 stack.2
  12.1 10.0 %all-to-all-start = ((bf16[32,128,512]{1,2,0:T(8,128)(2,1)}), bf16[32,128,512]{1,2,0:T(8,128)(2,1)}, u32[]{:S(2)}, u32[]{:S(2)}) async-start(bf16[32,128,512]{1,2,0:T(8,128)(2,1)} %stack.2), calls=%async_computation | async-start | bytes 8388608 | tf_op jit(solution)/shard_map/all_to_all | solution.py:38
  22.2 1.0 copy.46
  23.1 0.5 reshape.146
  23.7 0.3 convolution_convert_fusion
  24.1 0.3 fusion.98
  24.4 0.2 fusion.94
  25.3 0.6 copy.38
  26.1 1.0 gather_fusion
  27.1 0.3 fusion.100
  27.4 2.4 convert_multiply_fusion.2
  29.8 89.0 %all-to-all-done = bf16[32,128,512]{1,2,0:T(8,128)(2,1)} async-done(((bf16[32,128,512]{1,2,0:T(8,128)(2,1)}), bf16[32,128,512]{1,2,0:T(8,128)(2,1)}, u32[]{:S(2)}, u32[]{:S(2)}) %all-to-all-start) | async-done | bytes 4194336 | tf_op jit(solution)/shard_map/all_to_all | solution.py:38
  118.8 6.9 copy.41
  125.6 7.7 %reshape_reshape.7 = bf16[4096,8,64]{0,2,1:T(8,128)(2,1)} reshape(bf16[32,128,512]{1,0,2:T(8,128)(2,1)} %copy.41) | data formatting | bytes 8388608 | tf_op jit(solution)/shard_map/reshape;reshape | solution.py:43
  133.4 3.9 fusion.99
  137.4 0.2 fusion.38
  137.7 9.5 %fusion.23 = f32[16,8,128]{2,1,0:T(8,128)S(1)} fusion(f32[16,128,128]{2,1,0:T(8,128)} %convert_multiply_fusion.2, f32[16,8,128]{2,1,0:T(8,128)S(1)} %copy.42, f32[16,8,128]{2,1,0:T(8,128)S(1)} %copy.39), kind=kLoop, calls=%fused_computation.33 | loop fusion | flops 25149440 | bytes 1245184 | tf_op jit(solution)/shard_map/while/body/eval_jaxpr/reduce_sum | solution.py:101
  147.2 0.1 convolution_bitcast_fusion.2
  147.4 4.3 gather_fusion.1
  151.7 9.5 %fusion.27 = f32[16,128,8,64]{1,3,2,0:T(8,128)S(1)} fusion(f32[16,128,128]{2,1,0:T(8,128)} %convert_multiply_fusion.2, f32[16,8,128]{2,1,0:T(8,128)} %copy-done.9, f32[16,8,128]{2,1,0:T(8,128)} %copy-done.7, bf16[16,128,8,64]{1,3,2,0:T(8,128)(2,1)} %gather_fusion.1, pred[16]{0:T(512)(128)(4,1)S(1)} %get-tuple-element.104), kind=kOutput, calls=%fused_computation.35 | convolution fusion | flops 294649856 | bytes 7471120 | tf_op jit(solution)/shard_map/while/body/eval_jaxpr/ghij,gjhk->gihk/dot_general | solution.py:94
  161.2 5.0 fusion.14
  166.2 2.6 reshape.106
  168.8 1.6 fusion.33
  170.5 0.2 fusion.89
  170.7 0.2 fusion.91
  171.0 12.0 %fusion.24 = f32[16,128,8,64]{1,3,2,0:T(8,128)S(1)} fusion(f32[16,8,128]{2,1,0:T(8,128)S(1)} %copy.44, f32[16,128,128]{2,1,0:T(8,128)} %convert_multiply_fusion.2, f32[16,8,128]{2,1,0:T(8,128)} %copy-done.9, f32[16,8,128]{2,1,0:T(8,128)} %copy-done.7, bf16[16,128,8,64]{1,3,2,0:T(8,128)(2,1)S(1)} %gather_fusion, pred[16]{0:T(512)(128)(4,1)S(1)} %get-tuple-element.105), kind=kOutput, calls=%fused_computation.34 | convolution fusion | flops 296747008 | bytes 7536656 | tf_op jit(solution)/shard_map/while/body/eval_jaxpr/ghij,gihk->gjhk/dot_general | solution.py:145
  183.1 16.1 %fusion.96 = (f32[16,8,128]{2,1,0:T(8,128)}, f32[16,8,128]{2,1,0:T(8,128)S(1)}) fusion(f32[16,8,128]{2,1,0:T(8,128)S(1)} %copy.48, bf16[16,128,8,64]{1,3,2,0:T(8,128)(2,1)S(1)} %copy-done.1, pred[16]{0:T(512)(128)(4,1)S(1)} %get-tuple-element.104, bf16[16,128,8,64]{1,3,2,0:T(8,128)(2,1)S(1)} %gather_fusion, pred[16]{0:T(512)(128)(4,1)S(1)} %get-tuple-element.105, ...), kind=kOutput, calls=%fused_computation.128 | convolution fusion | flops 316637184 | bytes 5636128 | tf_op jit(solution)/shard_map/while/body/eval_jaxpr/gihk,gjhk->ghij/dot_general | solution.py:138
  199.2 0.3 fusion.42
  199.6 5.8 fusion.16
  205.4 12.0 %bitcast_add_fusion = f32[4096,512]{0,1:T(8,128)} fusion(f32[64,8,32,128]{3,2,1,0:T(8,128)S(1)} %bitcast.178, f32[512]{0:T(512)S(1)} %mul.185, f32[4096,8]{0,1:T(8,128)S(1)} %bitcast.183), kind=kLoop, calls=%fused_computation.22 | loop fusion | flops 4194304 | bytes 16910336 | tf_op jit(solution)/shard_map/add | solution.py:183
  217.6 0.7 copy-done.6
  218.3 0.1 convolution_bitcast_fusion.1
  218.5 0.3 fusion.34
  218.8 0.5 fusion.59
  219.3 0.6 convolution_bitcast_fusion
  219.9 5.1 fusion.103
  225.0 119.2 %reduce-scatter.2.cloned.1.call-done = f32[128,512]{0,1:T(8,128)} async-done(((f32[4096,512]{0,1:T(8,128)}), f32[128,512]{0,1:T(8,128)}) %reduce-scatter.2.cloned.1.call-update) | async-done | bytes 262160 | tf_op jit(solution)/shard_map/reduce_scatter | solution.py:195
  344.2 0.5 fusion.57
  344.7 75.2 %all-reduce = (f32[8,64]{1,0:T(8,128)}, f32[8,64]{1,0:T(8,128)}) all-reduce(f32[8,64]{1,0:T(8,128)S(1)} %add.168, f32[8,64]{1,0:T(8,128)S(1)} %bitcast.197), channel_id=1, replica_groups=mesh['panel'=32,'rep'=8] {'panel','rep'}, use_global_device_ids=true, to_apply=%region_8.10 | all-reduce | flops 1024 | bytes 8192 | tf_op jit(solution)/shard_map/psum | solution.py:201
  419.9 1.7 fusion.102
  421.6 11.8 %all-reduce.4.cloned.1.call-done = f32[128,512]{0,1:T(8,128)} async-done(((f32[128,512]{0,1:T(8,128)}), f32[128,512]{0,1:T(8,128)}) %all-reduce.4.cloned.1.call-update) | async-done | bytes 262160 | tf_op jit(solution)/shard_map/psum | solution.py:196
  433.4 2.0 convolution_add_fusion
  435.5 2.0 fusion.101
  437.4 252.4 %all-reduce.6.cloned.1.call-done = f32[128,512]{0,1:T(8,128)} async-done(((f32[128,512]{0,1:T(8,128)}), f32[128,512]{0,1:T(8,128)}) %all-reduce.6.cloned.1.call-update) | async-done | bytes 262160 | tf_op jit(solution)/shard_map/psum | solution.py:201
  689.8 1.8 copy.52
  (57 shorter events, 0.8 us)
Async XLA Ops:
  7.2 0.9 copy-start
  7.2 15.0 %copy-start.3 = (bf16[512,512]{1,0:T(8,128)(2,1)S(1)}, bf16[512,512]{1,0:T(8,128)(2,1)}, u32[]{:S(2)}) copy-start(bf16[512,512]{1,0:T(8,128)(2,1)} %param.17) | copy-start | bytes 1572868
  7.2 16.5 %copy-start.5 = (bf16[512,128]{1,0:T(8,128)(2,1)S(1)}, bf16[512,128]{1,0:T(8,128)(2,1)}, u32[]{:S(2)}) copy-start(bf16[512,128]{1,0:T(8,128)(2,1)} %param.13) | copy-start | bytes 393220
  7.2 16.8 %copy-start.13 = (f32[8,64]{1,0:T(8,128)S(1)}, f32[8,64]{1,0:T(8,128)}, u32[]{:S(2)}) copy-start(f32[8,64]{1,0:T(8,128)} %param.16) | copy-start | bytes 6148
  9.1 15.3 %copy-start.12 = (s32[16]{0:T(128)S(1)}, s32[16]{0:T(128)}, u32[]{:S(2)}) copy-start(s32[16]{0:T(128)} %param.18) | copy-start | bytes 196
  9.1 16.8 %copy-start.11 = (f32[8,64]{1,0:T(8,128)S(1)}, f32[8,64]{1,0:T(8,128)}, u32[]{:S(2)}) copy-start(f32[8,64]{1,0:T(8,128)} %param.15) | copy-start | bytes 6148
  12.1 106.7 %all-to-all-start = ((bf16[32,128,512]{1,2,0:T(8,128)(2,1)}), bf16[32,128,512]{1,2,0:T(8,128)(2,1)}, u32[]{:S(2)}, u32[]{:S(2)}) async-start(bf16[32,128,512]{1,2,0:T(8,128)(2,1)} %stack.2), calls=%async_computation | async-start | bytes 8388608 | tf_op jit(solution)/shard_map/all_to_all | solution.py:38
  22.1 4.9 copy-start.14
  22.1 322.0 %reduce-scatter.2.cloned.1.call-start = ((), (), s32[]{:S(2)}) async-start(), calls=%async_computation.2 | async-start | bytes 8650752 | tf_op jit(solution)/shard_map/reduce_scatter | solution.py:195
  24.7 113.0 %copy-start.7 = (f32[16,8,128]{2,1,0:T(8,128)}, f32[16,8,128]{2,1,0:T(8,128)S(1)}, u32[]{:S(2)}) copy-start(f32[16,8,128]{2,1,0:T(8,128)S(1)} %copy.39) | copy-start | bytes 196612
  137.7 14.1 %copy-start.9 = (f32[16,8,128]{2,1,0:T(8,128)}, f32[16,8,128]{2,1,0:T(8,128)S(1)}, u32[]{:S(2)}) copy-start(f32[16,8,128]{2,1,0:T(8,128)S(1)} %copy.42) | copy-start | bytes 196612
  151.7 17.1 %copy-start.2 = (bf16[512,512]{0,1:T(8,128)(2,1)S(1)}, bf16[512,512]{0,1:T(8,128)(2,1)}, u32[]{:S(2)}) copy-start(bf16[512,512]{0,1:T(8,128)(2,1)} %copy.46) | copy-start | bytes 1572868
  171.0 12.1 %copy-start.1 = (bf16[16,128,8,64]{1,3,2,0:T(8,128)(2,1)S(1)}, bf16[16,128,8,64]{1,3,2,0:T(8,128)(2,1)}, u32[]{:S(2)}) copy-start(bf16[16,128,8,64]{1,3,2,0:T(8,128)(2,1)} %gather_fusion.1) | copy-start | bytes 6291460
  171.0 12.1 %copy-start.4 = (f32[16,128,128]{2,1,0:T(8,128)S(1)}, f32[16,128,128]{2,1,0:T(8,128)}, u32[]{:S(2)}) copy-start(f32[16,128,128]{2,1,0:T(8,128)} %convert_multiply_fusion.2) | copy-start | bytes 3145732
  171.0 12.1 %copy-start.8 = (f32[16,8,128]{2,1,0:T(8,128)S(1)}, f32[16,8,128]{2,1,0:T(8,128)}, u32[]{:S(2)}) copy-start(f32[16,8,128]{2,1,0:T(8,128)} %copy-done.7) | copy-start | bytes 196612
  171.0 12.1 %copy-start.10 = (f32[16,8,128]{2,1,0:T(8,128)S(1)}, f32[16,8,128]{2,1,0:T(8,128)}, u32[]{:S(2)}) copy-start(f32[16,8,128]{2,1,0:T(8,128)} %copy-done.9) | copy-start | bytes 196612
  217.4 0.8 copy-start.6
  217.5 216.0 %all-reduce.4.cloned.1.call-start = ((), (), s32[]{:S(2)}) async-start(), calls=%async_computation.3 | async-start | bytes 524288 | tf_op jit(solution)/shard_map/psum | solution.py:196
  344.2 345.7 %all-reduce.6.cloned.1.call-start = ((), (), s32[]{:S(2)}) async-start(), calls=%async_computation.4 | async-start | bytes 524288 | tf_op jit(solution)/shard_map/psum | solution.py:201
Sparse Core Ops, SparseCore 0:
  217.6 126.5 reduce-scatter.1
  346.7 86.6 all-reduce.3
  440.4 249.4 all-reduce.5
